TPU v7x, 512 devices: a whole 4x8x8 slice. The times are simulated.
512 devices in a mesh: ctx: 64 (over z_lo, y, core), head: 8 (over z_hi, x).
Axes of the slice: x: 4, y: 8, z: 8 (z_hi: 2, z_lo: 4; z = z_hi * 4 + z_lo), core: 2. Of those that a mesh axis runs over, the one named last changes fastest.
Arguments:
- frozen_queries: bfloat16 [8192, 12288], P('ctx', 'head'), may hold values from -20.4 to 20.4
- query_latent_rows: bfloat16 [8192, 1536], P('ctx'), may hold values from -6 to 6
- key_value_latent: bfloat16 [8192, 576], P('ctx'), may hold values from -20.4 to 20.4
- block_starts: int32 [64, 2], P('ctx'), may hold values from 0 to 960, as said below
- latent_up_weight: bfloat16 [512, 16384], P(None, 'head'), may hold values from -0.25 to 0.25
- query_adapter_first: bfloat16 [1536, 32], replicated, may hold values from -0.15625 to 0.15625
- query_adapter_second: bfloat16 [32, 12288], P(None, 'head'), may hold values from -1 to 1
- output_adapter_first: bfloat16 [8192, 32], P('head'), may hold values from -0.0625 to 0.0625
- output_adapter_second: bfloat16 [32, 2560], replicated, may hold values from -1 to 1
- frozen_output_weight: bfloat16 [8192, 2560], P('head', 'ctx'), may hold values from -0.0625 to 0.0625
- output_cotangent: bfloat16 [8192, 2560], P('ctx'), may hold values from -0.1875 to 0.1875
Outputs:
- grad_qa: float32 [1536, 32], replicated
- grad_qb: float32 [32, 12288], P(None, 'head')
- grad_oa: float32 [8192, 32], P('head')
- grad_ob: float32 [32, 2560], P(None, 'ctx')
Inputs may be any that keep to these rules, and one draw needn't show every extreme that they name: For c < 8, each of the 8 groups of one sequence holds block_starts = (c * 64, (15 - c) * 64), every c once per sequence.
All inputs are finite; a program needn't handle non-finite values.
Results may differ from a plain program's by a relative error of at most 0.02.
The roundings to bfloat16 on the way count: a program that leaves them out, or rounds other values in their place, can miss the bound.
Values may be sent and summed in bfloat16 or wider, within the bound.
A program may use at most 128 MiB of HBM per device.

v0:
```python
import jax
import jax.numpy as jnp
from jax import lax
from jax.sharding import PartitionSpec as P

PLAIN_WIDTH = 128
ROTARY_WIDTH = 64
VALUE_WIDTH = 128
KVL = 512
SPAN = 8
ROPE_BASE = 10000.0


def passed_along(value, axis, steps):
    count = lax.axis_size(axis)
    pairs = [(source, (source + steps) % count) for source in range(count)]
    return lax.ppermute(value, axis, pairs)


def rotate(vectors, positions, sign):
    half_width = vectors.shape[-1] // 2
    freq = ROPE_BASE ** (-jnp.arange(half_width, dtype=jnp.float32) * 2.0 / vectors.shape[-1])
    angle = positions.astype(jnp.float32)[..., None] * freq
    angle = angle.reshape(
        positions.shape + (1,) * (vectors.ndim - positions.ndim - 1) + (half_width,)
    )
    cosine = jnp.cos(angle)
    sine = jnp.sin(angle) * sign
    first = vectors[..., :half_width]
    second = vectors[..., half_width:]
    return jnp.concatenate([first * cosine - second * sine, second * cosine + first * sine], -1)


def block_positions(offsets, half_rows):
    steps = jnp.arange(half_rows, dtype=jnp.int32)
    return jnp.concatenate([offsets[0] + steps, offsets[1] + steps])


def expand_block(latent_rows, latent_up_weight, positions):
    kv_up = jnp.dot(
        latent_rows[:, :KVL], latent_up_weight, preferred_element_type=jnp.float32
    ).astype(jnp.bfloat16)
    rope_key = rotate(latent_rows[:, KVL:].astype(jnp.float32), positions, 1.0).astype(jnp.bfloat16)
    return jnp.concatenate([kv_up, rope_key], -1)


def block_scores(query_full, block, head_number):
    split = head_number * (PLAIN_WIDTH + VALUE_WIDTH)
    kv_heads = block[:, :split].reshape(block.shape[0], head_number, PLAIN_WIDTH + VALUE_WIDTH)
    nope_part = jnp.einsum(
        "qhd,khd->hqk",
        query_full[..., :PLAIN_WIDTH],
        kv_heads[..., :PLAIN_WIDTH],
        preferred_element_type=jnp.float32,
    )
    rope_part = jnp.einsum(
        "qhd,kd->hqk",
        query_full[..., PLAIN_WIDTH:],
        block[:, split:],
        preferred_element_type=jnp.float32,
    )
    return nope_part + rope_part


def contract_rows(left, right):
    return lax.dot_general(
        left, right, (((0,), (0,)), ((), ())), preferred_element_type=jnp.float32
    )


def columns_contract(left, right):
    return lax.dot_general(
        left, right, (((1,), (1,)), ((), ())), preferred_element_type=jnp.float32
    )


def body(
    frozen_queries,
    query_latent_rows,
    key_value_latent,
    block_starts,
    latent_up_weight,
    query_adapter_first,
    query_adapter_second,
    output_adapter_first,
    output_adapter_second,
    frozen_output_weight,
    output_cotangent,
):
    token_rows = frozen_queries.shape[0]
    half_rows = token_rows // 2
    per_head_width = PLAIN_WIDTH + ROTARY_WIDTH
    head_number = query_adapter_second.shape[1] // per_head_width
    score_scale = per_head_width ** (-0.5)
    axis_count = lax.axis_size("ctx")
    stride = axis_count // SPAN
    axis_place = lax.axis_index("ctx")
    all_offsets = lax.all_gather(block_starts, "ctx", axis=0, tiled=True)
    own_positions = block_positions(block_starts[0], half_rows)
    query_rank_rows = jnp.dot(
        query_latent_rows, query_adapter_first, preferred_element_type=jnp.float32
    ).astype(jnp.bfloat16)
    query_full = frozen_queries.astype(jnp.float32) + jnp.dot(
        query_rank_rows, query_adapter_second, preferred_element_type=jnp.float32
    )
    query_full = query_full.reshape(token_rows, head_number, per_head_width)
    query_full = jnp.concatenate(
        [query_full[..., :PLAIN_WIDTH], rotate(query_full[..., PLAIN_WIDTH:], own_positions, 1.0)],
        -1,
    ).astype(jnp.bfloat16)

    def prepare(block, positions):
        return expand_block(block, latent_up_weight, positions)

    collected = []

    def take(block, distance):
        source = (axis_place - distance * stride) % axis_count
        source_offsets = lax.dynamic_index_in_dim(all_offsets, source, 0, keepdims=False)
        positions = block_positions(source_offsets, half_rows)
        expanded = prepare(block, positions)
        collected.append((expanded, positions, block_scores(query_full, expanded, head_number)))

    take(key_value_latent, 0)
    moving = key_value_latent
    for hop in range(1, SPAN):
        moving = passed_along(moving, "ctx", stride)
        take(moving, hop)
    kv_all = jnp.concatenate([entry[0] for entry in collected], 0)
    key_positions = jnp.concatenate([entry[1] for entry in collected], 0)
    scores = jnp.concatenate([entry[2] for entry in collected], -1) * score_scale
    causal = key_positions[None, :] <= own_positions[:, None]
    scores = jnp.where(causal[None], scores, -jnp.inf)
    top = jnp.max(scores, -1, keepdims=True)
    expo = jnp.exp(scores - top)
    weights = (expo / jnp.sum(expo, -1, keepdims=True)).astype(jnp.bfloat16)
    split = head_number * (PLAIN_WIDTH + VALUE_WIDTH)
    key_count = kv_all.shape[0]
    kv_heads = kv_all[:, :split].reshape(key_count, head_number, PLAIN_WIDTH + VALUE_WIDTH)
    key_nope = kv_heads[..., :PLAIN_WIDTH]
    values = kv_heads[..., PLAIN_WIDTH:]
    rope_keys = kv_all[:, split:]
    attended_values = jnp.einsum(
        "hqk,khv->qhv", weights, values, preferred_element_type=jnp.float32
    ).astype(jnp.bfloat16)
    attended_flattened = attended_values.reshape(token_rows, head_number * VALUE_WIDTH)
    output_partial_sum = jnp.dot(
        attended_flattened, output_adapter_first, preferred_element_type=jnp.float32
    )
    output_rank_rows = lax.psum(output_partial_sum, "head").astype(jnp.bfloat16)
    output_rank_gradient = columns_contract(output_cotangent, output_adapter_second).astype(
        jnp.bfloat16
    )
    grad_ob = lax.psum_scatter(
        contract_rows(output_rank_rows, output_cotangent), "ctx", scatter_dimension=1, tiled=True
    )
    grad_oa = lax.psum(contract_rows(attended_flattened, output_rank_gradient), "ctx")
    frozen_query_gradient = columns_contract(
        output_cotangent, lax.all_gather(frozen_output_weight, "ctx", axis=1, tiled=True)
    )
    attended_gradient = (
        (frozen_query_gradient + columns_contract(output_rank_gradient, output_adapter_first))
        .astype(jnp.bfloat16)
        .reshape(token_rows, head_number, VALUE_WIDTH)
    )
    d_prob = jnp.einsum(
        "qhv,khv->hqk", attended_gradient, values, preferred_element_type=jnp.float32
    )
    weights_wide = weights.astype(jnp.float32)
    delta = jnp.sum(weights_wide * d_prob, -1, keepdims=True)
    d_score = (weights_wide * (d_prob - delta) * score_scale).astype(jnp.bfloat16)
    dq_nope = jnp.einsum("hqk,khd->qhd", d_score, key_nope, preferred_element_type=jnp.float32)
    dq_rope = jnp.einsum("hqk,kd->qhd", d_score, rope_keys, preferred_element_type=jnp.float32)
    dq_rope = rotate(dq_rope, own_positions, -1.0)
    query_gradient = (
        jnp.concatenate([dq_nope, dq_rope], -1)
        .reshape(token_rows, head_number * per_head_width)
        .astype(jnp.bfloat16)
    )
    qb_term = contract_rows(query_rank_rows, query_gradient)
    query_adapter_gradient = lax.psum(
        columns_contract(query_gradient, query_adapter_second), "head"
    ).astype(jnp.bfloat16)
    qa_term = contract_rows(query_latent_rows, query_adapter_gradient)
    grad_qb, grad_qa = lax.psum((qb_term, qa_term), "ctx")
    return (grad_qa, grad_qb, grad_oa, grad_ob)


def solution(mesh):
    return jax.shard_map(
        body,
        mesh=mesh,
        in_specs=(
            P("ctx", "head"),
            P("ctx", None),
            P("ctx", None),
            P("ctx", None),
            P(None, "head"),
            P(),
            P(None, "head"),
            P("head", None),
            P(),
            P("head", "ctx"),
            P("ctx", None),
        ),
        out_specs=(P(), P(None, "head"), P("head", None), P(None, "ctx")),
        check_vma=False,
    )
```

profile of v0, /device:TPU:1, one launch (start us, length us, event | category | flops | bytes accessed | tf_op | source)
XLA Modules:
  0.0 902.7 jit_solution(16338640068785759681)
XLA Ops:
  7.3 8.5 collective-permute-start
  24.4 80.7 %all-gather = s32[64,1,2]{2,1,0:T(1,128)} all-gather(s32[1,1,2]{2,1,0:T(1,128)S(1)} %bitcast.209), channel_id=1, replica_groups=mesh['ctx'=64,'head'=8] {'ctx'}, dimensions={0}, use_global_device_ids=true | all-gather | bytes 520 | tf_op jit(solution)/shard_map/all_gather | solution.py:98
  123.5 2.0 fusion.62
  145.4 1.9 constant_dynamic-update-slice_fusion.7
  150.6 2.0 constant_dynamic-update-slice_fusion.6
  152.6 1.9 collective-permute-start.1
  154.5 2.0 fusion.60
  156.5 10.0 %collective-permute-done.1 = bf16[128,576]{0,1:T(8,128)(2,1)S(1)} collective-permute-done((bf16[128,576]{0,1:T(8,128)(2,1)}, bf16[128,576]{0,1:T(8,128)(2,1)S(1)}, u32[]{:S(2)}, u32[]{:S(2)}) %collective-permute-start.1) | collective-permute-done | bytes 147488 | tf_op jit(solution)/shard_map/ppermute | solution.py:17
  168.2 1.9 collective-permute-start.2
  170.2 11.2 %collective-permute-done.2 = bf16[128,576]{0,1:T(8,128)(2,1)S(1)} collective-permute-done((bf16[128,576]{0,1:T(8,128)(2,1)S(1)}, bf16[128,576]{0,1:T(8,128)(2,1)S(1)}, u32[]{:S(2)}, u32[]{:S(2)}) %collective-permute-start.2) | collective-permute-done | bytes 147488 | tf_op jit(solution)/shard_map/ppermute | solution.py:17
  183.1 1.9 collective-permute-start.3
  185.0 11.9 %collective-permute-done.3 = bf16[128,576]{0,1:T(8,128)(2,1)S(1)} collective-permute-done((bf16[128,576]{0,1:T(8,128)(2,1)S(1)}, bf16[128,576]{0,1:T(8,128)(2,1)S(1)}, u32[]{:S(2)}, u32[]{:S(2)}) %collective-permute-start.3) | collective-permute-done | bytes 147488 | tf_op jit(solution)/shard_map/ppermute | solution.py:17
  207.0 1.9 concatenate.151
  210.7 1.9 concatenate.155
  212.6 1.9 collective-permute-start.4
  214.5 1.9 constant_dynamic-update-slice_fusion.5
  216.5 1.9 constant_dynamic-update-slice_fusion.4
  218.4 1.9 constant_dynamic-update-slice_fusion.3
  220.3 1.9 fusion.54
  222.3 3.1 collective-permute-done.4
  226.0 1.9 collective-permute-start.5
  228.9 10.8 %collective-permute-done.5 = bf16[128,576]{0,1:T(8,128)(2,1)S(1)} collective-permute-done((bf16[128,576]{0,1:T(8,128)(2,1)S(1)}, bf16[128,576]{0,1:T(8,128)(2,1)S(1)}, u32[]{:S(2)}, u32[]{:S(2)}) %collective-permute-start.5) | collective-permute-done | bytes 147488 | tf_op jit(solution)/shard_map/ppermute | solution.py:17
  240.4 1.9 collective-permute-start.6
  243.4 9.6 %collective-permute-done.6 = bf16[128,576]{0,1:T(8,128)(2,1)S(1)} collective-permute-done((bf16[128,576]{0,1:T(8,128)(2,1)S(1)}, bf16[128,576]{0,1:T(8,128)(2,1)S(1)}, u32[]{:S(2)}, u32[]{:S(2)}) %collective-permute-start.6) | collective-permute-done | bytes 147488 | tf_op jit(solution)/shard_map/ppermute | solution.py:17
  262.6 2.5 slice.337
  271.0 1.9 fusion.188
  277.3 3.3 fusion.197
  280.9 2.7 fusion.16
  283.6 6.7 fusion.42
  290.4 7.4 fusion.43
  300.0 50.8 %all-reduce.2 = (bf16[128,32]{0,1:T(8,128)(2,1)S(1)}, bf16[128,32]{0,1:T(8,128)(2,1)S(1)}) all-reduce(f32[128,32]{0,1:T(8,128)S(1)} %fusion.200, f32[128,32]{0,1:T(8,128)} %fusion.201), channel_id=1, replica_groups=mesh['ctx'=64,'head'=8] {'head'}, use_global_device_ids=true, to_apply=%region_3.4 | all-reduce | flops 8192 | bytes 49152 | tf_op jit(solution)/shard_map/psum | solution.py:181
  354.6 535.1 %all-reduce.5.cloned.1.call-done = (f32[1536,32]{0,1:T(8,128)}, f32[32,1536]{1,0:T(8,128)}, f32[1024,32]{0,1:T(8,128)}, f32[32,2560]{1,0:T(8,128)}) async-done(((f32[1536,32]{0,1:T(8,128)}, f32[32,1536]{1,0:T(8,128)}, f32[1024,32]{0,1:T(8,128)}, f32[32,2560]{1,0:T(8,128)}), (f32[1536,32]{0,1:T(8,128)}, f32[32,1536]{1,0:T(8,128)}, f32[1024,32]{0,1:T(8,128)}, ...) | async-done | bytes 851984 | tf_op jit(solution)/shard_map/psum | solution.py:185
  (297 shorter events, 99.3 us)
Async XLA Ops:
  7.2 16.6 %copy-start.62 = (s32[1,2]{1,0:T(1,128)S(1)}, s32[1,2]{1,0:T(1,128)}, u32[]{:S(2)}) copy-start(s32[1,2]{1,0:T(1,128)} %param.14) | copy-start | bytes 28
  7.2 270.1 %all-gather.3.cloned.1.call-start = ((), (), s32[]{:S(2)}) async-start(), calls=%async_computation | async-start | bytes 5324800 | tf_op jit(solution)/shard_map/all_gather | solution.py:159
  7.3 128.1 %collective-permute-start = (bf16[128,576]{0,1:T(8,128)(2,1)}, bf16[128,576]{0,1:T(8,128)(2,1)}, u32[]{:S(2)}, u32[]{:S(2)}) collective-permute-start(bf16[128,576]{0,1:T(8,128)(2,1)} %param.13), channel_id=1, source_target_pairs={{0,64},{8,72},{16,80},{24,88},{32,96},{40,104},{48,112},{56,120},{... | collective-permute-start | bytes 442376 | tf_op jit(solution)/shard_map/ppermute | solution.py:17
  15.8 873.8 %all-reduce.5.cloned.1.call-start = ((), (), s32[]{:S(2)}) async-start(), calls=%async_computation.1 | async-start | bytes 1703936 | tf_op jit(solution)/shard_map/psum | solution.py:185
  18.0 113.1 %copy-start.2 = (bf16[128,2560]{1,0:T(8,128)(2,1)S(1)}, bf16[128,2560]{1,0:T(8,128)(2,1)}, u32[]{:S(2)}) copy-start(bf16[128,2560]{1,0:T(8,128)(2,1)} %param.21) | copy-start | bytes 1966084
  109.0 19.7 %copy-start.70 = (s32[64]{0:T(128)}, s32[64]{0:T(128)S(1)}, u32[]{:S(2)}) copy-start(s32[64]{0:T(128)S(1)} %iota_add_fusion.14) | copy-start | bytes 772
  109.6 19.1 %copy-start.71 = (s32[64]{0:T(128)}, s32[64]{0:T(128)S(1)}, u32[]{:S(2)}) copy-start(s32[64]{0:T(128)S(1)} %iota_add_fusion.15) | copy-start | bytes 772
  110.9 17.8 %copy-start.78 = (s32[64]{0:T(128)}, s32[64]{0:T(128)S(1)}, u32[]{:S(2)}) copy-start(s32[64]{0:T(128)S(1)} %iota_add_fusion.2) | copy-start | bytes 772
  111.5 17.2 %copy-start.79 = (s32[64]{0:T(128)}, s32[64]{0:T(128)S(1)}, u32[]{:S(2)}) copy-start(s32[64]{0:T(128)S(1)} %iota_add_fusion.3) | copy-start | bytes 772
  112.8 15.9 %copy-start.72 = (s32[64]{0:T(128)}, s32[64]{0:T(128)S(1)}, u32[]{:S(2)}) copy-start(s32[64]{0:T(128)S(1)} %iota_add_fusion.6) | copy-start | bytes 772
  113.5 15.3 %copy-start.73 = (s32[64]{0:T(128)}, s32[64]{0:T(128)S(1)}, u32[]{:S(2)}) copy-start(s32[64]{0:T(128)S(1)} %iota_add_fusion.7) | copy-start | bytes 772
  140.7 26.3 %copy-start.32 = (bf16[128,32]{0,1:T(8,128)(2,1)}, bf16[128,32]{0,1:T(8,128)(2,1)S(1)}, u32[]{:S(2)}) copy-start(bf16[128,32]{0,1:T(8,128)(2,1)S(1)} %get-tuple-element.30) | copy-start | bytes 24580
  140.7 26.3 %copy-start.34 = (bf16[128,32]{0,1:T(8,128)(2,1)}, bf16[128,32]{0,1:T(8,128)(2,1)S(1)}, u32[]{:S(2)}) copy-start(bf16[128,32]{0,1:T(8,128)(2,1)S(1)} %get-tuple-element.31) | copy-start | bytes 24580
  152.6 13.9 %collective-permute-start.1 = (bf16[128,576]{0,1:T(8,128)(2,1)}, bf16[128,576]{0,1:T(8,128)(2,1)S(1)}, u32[]{:S(2)}, u32[]{:S(2)}) collective-permute-start(bf16[128,576]{0,1:T(8,128)(2,1)} %collective-permute-done), channel_id=1, source_target_pairs={{0,64},{8,72},{16,80},{24,88},{32,96},{40,104},{48,112},{56,120},{... | collective-permute-start | bytes 442376 | tf_op jit(solution)/shard_map/ppermute | solution.py:17
  167.0 16.1 %copy-start.5 = (bf16[128,2048]{1,0:T(8,128)(2,1)}, bf16[128,2048]{1,0:T(8,128)(2,1)S(1)}, u32[]{:S(2)}) copy-start(bf16[128,2048]{1,0:T(8,128)(2,1)S(1)} %convolution_convert_fusion.5) | copy-start | bytes 1572868
  168.2 13.1 %collective-permute-start.2 = (bf16[128,576]{0,1:T(8,128)(2,1)S(1)}, bf16[128,576]{0,1:T(8,128)(2,1)S(1)}, u32[]{:S(2)}, u32[]{:S(2)}) collective-permute-start(bf16[128,576]{0,1:T(8,128)(2,1)S(1)} %collective-permute-done.1), channel_id=1, source_target_pairs={{0,64},{8,72},{16,80},{24,88},{32,96},{40,104},{48,112},{56,120},{... | collective-permute-start | bytes 442376 | tf_op jit(solution)/shard_map/ppermute | solution.py:17
  181.8 17.1 %copy-start.60 = (f32[32]{0:T(128)S(1)}, f32[32]{0:T(128)}, u32[]{:S(2)}) copy-start(f32[32]{0:T(128)} %multiply_power_fusion) | copy-start | bytes 388
  181.8 17.1 %copy-start.66 = (f32[128]{0:T(128)S(1)}, f32[128]{0:T(128)}, u32[]{:S(2)}) copy-start(f32[128]{0:T(128)} %get-tuple-element.79) | copy-start | bytes 1540
  181.8 17.1 %copy-start.67 = (f32[128]{0:T(128)S(1)}, f32[128]{0:T(128)}, u32[]{:S(2)}) copy-start(f32[128]{0:T(128)} %get-tuple-element.80) | copy-start | bytes 1540
  181.9 17.1 %copy-start.77 = (f32[128]{0:T(128)S(1)}, f32[128]{0:T(128)}, u32[]{:S(2)}) copy-start(f32[128]{0:T(128)} %add_convert_fusion.6) | copy-start | bytes 1540
  183.1 13.8 %collective-permute-start.3 = (bf16[128,576]{0,1:T(8,128)(2,1)S(1)}, bf16[128,576]{0,1:T(8,128)(2,1)S(1)}, u32[]{:S(2)}, u32[]{:S(2)}) collective-permute-start(bf16[128,576]{0,1:T(8,128)(2,1)S(1)} %collective-permute-done.2), channel_id=1, source_target_pairs={{0,64},{8,72},{16,80},{24,88},{32,96},{40,104},{48,112},{56,120},{... | collective-permute-start | bytes 442376 | tf_op jit(solution)/shard_map/ppermute | solution.py:17
  199.9 25.9 %copy-start.38 = (bf16[128,32]{0,1:T(8,128)(2,1)}, bf16[128,32]{0,1:T(8,128)(2,1)S(1)}, u32[]{:S(2)}) copy-start(bf16[128,32]{0,1:T(8,128)(2,1)S(1)} %get-tuple-element.24) | copy-start | bytes 24580
  199.9 25.9 %copy-start.40 = (bf16[128,32]{0,1:T(8,128)(2,1)}, bf16[128,32]{0,1:T(8,128)(2,1)S(1)}, u32[]{:S(2)}) copy-start(bf16[128,32]{0,1:T(8,128)(2,1)S(1)} %get-tuple-element.25) | copy-start | bytes 24580
  212.6 12.7 %collective-permute-start.4 = (bf16[128,576]{0,1:T(8,128)(2,1)}, bf16[128,576]{0,1:T(8,128)(2,1)S(1)}, u32[]{:S(2)}, u32[]{:S(2)}) collective-permute-start(bf16[128,576]{0,1:T(8,128)(2,1)} %copy-done.25), channel_id=1, source_target_pairs={{0,64},{8,72},{16,80},{24,88},{32,96},{40,104},{48,112},{56,120},{... | collective-permute-start | bytes 442376 | tf_op jit(solution)/shard_map/ppermute | solution.py:17
  225.8 17.6 %copy-start.4 = (bf16[128,2048]{1,0:T(8,128)(2,1)}, bf16[128,2048]{1,0:T(8,128)(2,1)S(1)}, u32[]{:S(2)}) copy-start(bf16[128,2048]{1,0:T(8,128)(2,1)S(1)} %convolution_convert_fusion.2) | copy-start | bytes 1572868
  226.0 13.8 %collective-permute-start.5 = (bf16[128,576]{0,1:T(8,128)(2,1)S(1)}, bf16[128,576]{0,1:T(8,128)(2,1)S(1)}, u32[]{:S(2)}, u32[]{:S(2)}) collective-permute-start(bf16[128,576]{0,1:T(8,128)(2,1)S(1)} %collective-permute-done.4), channel_id=1, source_target_pairs={{0,64},{8,72},{16,80},{24,88},{32,96},{40,104},{48,112},{56,120},{... | collective-permute-start | bytes 442376 | tf_op jit(solution)/shard_map/ppermute | solution.py:17
  240.2 14.2 %copy-start.61 = (f32[32]{0:T(128)S(1)}, f32[32]{0:T(128)}, u32[]{:S(2)}) copy-start(f32[32]{0:T(128)} %multiply_power_fusion) | copy-start | bytes 388
  240.2 14.2 %copy-start.63 = (f32[128]{0:T(128)S(1)}, f32[128]{0:T(128)}, u32[]{:S(2)}) copy-start(f32[128]{0:T(128)} %get-tuple-element.10) | copy-start | bytes 1540
  240.3 14.2 %copy-start.64 = (f32[128]{0:T(128)S(1)}, f32[128]{0:T(128)}, u32[]{:S(2)}) copy-start(f32[128]{0:T(128)} %get-tuple-element.81) | copy-start | bytes 1540
  240.4 12.6 %collective-permute-start.6 = (bf16[128,576]{0,1:T(8,128)(2,1)S(1)}, bf16[128,576]{0,1:T(8,128)(2,1)S(1)}, u32[]{:S(2)}, u32[]{:S(2)}) collective-permute-start(bf16[128,576]{0,1:T(8,128)(2,1)S(1)} %collective-permute-done.5), channel_id=1, source_target_pairs={{0,64},{8,72},{16,80},{24,88},{32,96},{40,104},{48,112},{56,120},{... | collective-permute-start | bytes 442376 | tf_op jit(solution)/shard_map/ppermute | solution.py:17
  290.4 60.4 %copy-start.20 = (bf16[128,1536]{1,0:T(8,128)(2,1)S(1)}, bf16[128,1536]{1,0:T(8,128)(2,1)}, u32[]{:S(2)}) copy-start(bf16[128,1536]{1,0:T(8,128)(2,1)} %param.12) | copy-start | bytes 1179652
  290.4 605.5 %copy-start.1 = (bf16[512,2048]{1,0:T(8,128)(2,1)S(1)}, bf16[512,2048]{1,0:T(8,128)(2,1)}, u32[]{:S(2)}) copy-start(bf16[512,2048]{1,0:T(8,128)(2,1)} %param.15) | copy-start | bytes 6291460
  (57 other events, 226.8 us)
Sparse Core Ops, SparseCore 0:
  15.9 122.1 all-gather.2
  352.8 536.8 all-reduce.4
where the time goes:
time: 905 us; the launch traced here: 903 us
  waiting for transfers between devices  592 us (65%)
  blocking collectives  131 us (14%)
  local copies, waits for them, and re-layouts  66.2 us (7%)
  matrix products  47 us (5%)
  other arithmetic  30 us (3%)
  starting transfers between devices  20.1 us (2%)
  between operations  16.3 us (2%)
    psum x1, waiting for transfers between devices, body(): grad_qb, grad_qa = lax.psum((qb_term, qa_term), 'ctx')  535 us
    all_gather x1, blocking collectives, body(): all_offsets = lax.all_gather(block_starts, 'ctx', axis=0, tiled=True)  80.7 us
    ppermute x7, waiting for transfers between devices, passed_along(): return lax.ppermute(value, axis, pairs)  56.6 us
    psum x1, blocking collectives, body(): lax.psum(columns_contract(query_gradient, query_adapter_second), 'head')  50.8 us
    unnamed x181, local copies, waits for them, and re-layouts  26.2 us
    ppermute x7, starting transfers between devices, passed_along(): return lax.ppermute(value, axis, pairs)  20 us
  transfers between devices with their start and end apart: 9, of which 7 were waited for; matrix products, arithmetic and copies ran while one was open for 12% of the time, Pallas kernels for 0%

commit v1 on v0

--- a/solution.py
+++ b/solution.py
@@ -95,7 +95,9 @@
     axis_count = lax.axis_size("ctx")
     stride = axis_count // SPAN
     axis_place = lax.axis_index("ctx")
-    all_offsets = lax.all_gather(block_starts, "ctx", axis=0, tiled=True)
+    all_offsets = jnp.concatenate(
+        lax.all_to_all(jnp.stack([block_starts] * lax.axis_size("ctx")), "ctx", 0, 0), axis=0
+    )
     own_positions = block_positions(block_starts[0], half_rows)
     query_rank_rows = jnp.dot(
         query_latent_rows, query_adapter_first, preferred_element_type=jnp.float32

time: 905 us -> 841 us (0.929)
  blocking collectives: 131 us -> 44.9 us
  starting transfers between devices: 20.1 us -> 38.6 us
    all_gather x1 -> x0, blocking collectives: 80.7 us -> none  [body(): all_offsets = lax.all_gather(block_starts, 'ctx', axis=0, tiled=True)]
    all_to_all x0 -> x1, starting transfers between devices: none -> 11.1 us  [body(): lax.all_to_all(jnp.stack([block_starts] * lax.axis_size('ctx')), 'ctx', 0...]
    unnamed x181 -> x175, local copies, waits for them, and re-layouts: 26.2 us -> 26.2 us
  transfers between devices with their start and end apart: 9 -> 10, of which waited for: 7 -> 7; matrix products, arithmetic and copies ran while one was open for 12% -> 13% of each run, Pallas kernels for 0% -> 0%
where the time goes in v1:
time: 841 us; the launch traced here: 839 us
  waiting for transfers between devices  591 us (70%)
  local copies, waits for them, and re-layouts  68.1 us (8%)
  matrix products  49.5 us (6%)
  blocking collectives  44.9 us (5%)
  starting transfers between devices  38.6 us (5%)
  other arithmetic  29.8 us (4%)
  between operations  16.3 us (2%)
    psum x1, waiting for transfers between devices, body(): grad_qb, grad_qa = lax.psum((qb_term, qa_term), 'ctx')  539 us
    ppermute x7, waiting for transfers between devices, passed_along(): return lax.ppermute(value, axis, pairs)  52 us
    psum x1, blocking collectives, body(): lax.psum(columns_contract(query_gradient, query_adapter_second), 'head')  44.9 us
    ppermute x7, starting transfers between devices, passed_along(): return lax.ppermute(value, axis, pairs)  27.4 us
    unnamed x175, local copies, waits for them, and re-layouts  26.2 us
  transfers between devices with their start and end apart: 10, of which 7 were waited for; matrix products, arithmetic and copies ran while one was open for 13% of the time, Pallas kernels for 0%

profile of v1, /device:TPU:1, one launch (start us, length us, event | category | flops | bytes accessed | tf_op | source)
XLA Modules:
  0.0 838.7 jit_solution(392956998926886347)
XLA Ops:
  7.2 8.4 %collective-permute-start = (bf16[128,576]{0,1:T(8,128)(2,1)}, bf16[128,576]{0,1:T(8,128)(2,1)}, u32[]{:S(2)}, u32[]{:S(2)}) collective-permute-start(bf16[128,576]{0,1:T(8,128)(2,1)} %param.13), channel_id=1, source_target_pairs={{0,64},{8,72},{16,80},{24,88},{32,96},{40,104},{48,112},{56,120},{... | collective-permute-start | bytes 442376 | tf_op jit(solution)/shard_map/ppermute | solution.py:17
  16.9 11.1 %all-to-all-start = ((s32[64,1,2]{2,1,0:T(1,128)}), s32[64,1,2]{2,1,0:T(1,128)}, u32[]{:S(2)}, u32[]{:S(2)}) async-start(s32[64,1,2]{2,1,0:T(1,128)} %stack.2), calls=%async_computation | async-start | bytes 65536 | tf_op jit(solution)/shard_map/all_to_all | solution.py:99
  38.0 2.0 fusion.62
  76.4 1.9 concatenate.147
  78.2 1.9 constant_dynamic-update-slice_fusion.7
  83.4 2.0 constant_dynamic-update-slice_fusion.6
  85.4 7.1 collective-permute-start.1
  92.6 2.0 fusion.60
  94.5 8.1 collective-permute-done.1
  104.3 4.2 collective-permute-start.2
  108.6 9.9 %collective-permute-done.2 = bf16[128,576]{0,1:T(8,128)(2,1)S(1)} collective-permute-done((bf16[128,576]{0,1:T(8,128)(2,1)S(1)}, bf16[128,576]{0,1:T(8,128)(2,1)S(1)}, u32[]{:S(2)}, u32[]{:S(2)}) %collective-permute-start.2) | collective-permute-done | bytes 147488 | tf_op jit(solution)/shard_map/ppermute | solution.py:17
  120.2 1.9 collective-permute-start.3
  122.1 10.9 %collective-permute-done.3 = bf16[128,576]{0,1:T(8,128)(2,1)S(1)} collective-permute-done((bf16[128,576]{0,1:T(8,128)(2,1)S(1)}, bf16[128,576]{0,1:T(8,128)(2,1)S(1)}, u32[]{:S(2)}, u32[]{:S(2)}) %collective-permute-start.3) | collective-permute-done | bytes 147488 | tf_op jit(solution)/shard_map/ppermute | solution.py:17
  146.8 1.9 concatenate.155
  148.7 1.9 collective-permute-start.4
  150.6 1.9 constant_dynamic-update-slice_fusion.5
  152.6 1.9 constant_dynamic-update-slice_fusion.4
  154.5 1.9 constant_dynamic-update-slice_fusion.3
  156.4 1.9 fusion.54
  158.3 3.3 collective-permute-done.4
  162.3 1.9 collective-permute-start.5
  165.2 9.6 %collective-permute-done.5 = bf16[128,576]{0,1:T(8,128)(2,1)S(1)} collective-permute-done((bf16[128,576]{0,1:T(8,128)(2,1)S(1)}, bf16[128,576]{0,1:T(8,128)(2,1)S(1)}, u32[]{:S(2)}, u32[]{:S(2)}) %collective-permute-start.5) | collective-permute-done | bytes 147488 | tf_op jit(solution)/shard_map/ppermute | solution.py:17
  175.4 1.9 collective-permute-start.6
  178.4 10.3 %collective-permute-done.6 = bf16[128,576]{0,1:T(8,128)(2,1)S(1)} collective-permute-done((bf16[128,576]{0,1:T(8,128)(2,1)S(1)}, bf16[128,576]{0,1:T(8,128)(2,1)S(1)}, u32[]{:S(2)}, u32[]{:S(2)}) %collective-permute-start.6) | collective-permute-done | bytes 147488 | tf_op jit(solution)/shard_map/ppermute | solution.py:17
  198.3 2.5 slice.337
  206.7 1.9 fusion.180
  213.0 3.3 fusion.189
  217.5 2.7 fusion.16
  220.2 6.0 fusion.42
  226.2 8.2 fusion.43
  238.1 44.9 %all-reduce.2 = (bf16[128,32]{0,1:T(8,128)(2,1)S(1)}, bf16[128,32]{0,1:T(8,128)(2,1)S(1)}) all-reduce(f32[128,32]{0,1:T(8,128)S(1)} %fusion.192, f32[128,32]{0,1:T(8,128)} %fusion.193), channel_id=1, replica_groups=mesh['ctx'=64,'head'=8] {'head'}, use_global_device_ids=true, to_apply=%region_3.4 | all-reduce | flops 8192 | bytes 49152 | tf_op jit(solution)/shard_map/psum | solution.py:183
  286.8 538.8 %all-reduce.5.cloned.1.call-done = (f32[1536,32]{0,1:T(8,128)}, f32[32,1536]{1,0:T(8,128)}, f32[1024,32]{0,1:T(8,128)}, f32[32,2560]{1,0:T(8,128)}) async-done(((f32[1536,32]{0,1:T(8,128)}, f32[32,1536]{1,0:T(8,128)}, f32[1024,32]{0,1:T(8,128)}, f32[32,2560]{1,0:T(8,128)}), (f32[1536,32]{0,1:T(8,128)}, f32[32,1536]{1,0:T(8,128)}, f32[1024,32]{0,1:T(8,128)}, ...) | async-done | bytes 851984 | tf_op jit(solution)/shard_map/psum | solution.py:187
  (293 shorter events, 104.2 us)
Async XLA Ops:
  7.2 25.0 %copy-start = (bf16[512,2048]{1,0:T(8,128)(2,1)S(1)}, bf16[512,2048]{1,0:T(8,128)(2,1)}, u32[]{:S(2)}) copy-start(bf16[512,2048]{1,0:T(8,128)(2,1)} %param.15) | copy-start | bytes 6291460
  7.2 27.3 %copy-start.27 = (bf16[1536,32]{0,1:T(8,128)(2,1)S(1)}, bf16[1536,32]{0,1:T(8,128)(2,1)}, u32[]{:S(2)}) copy-start(bf16[1536,32]{0,1:T(8,128)(2,1)} %param.16) | copy-start | bytes 294916
  7.2 28.2 %copy-start.22 = (bf16[32,1536]{1,0:T(8,128)(2,1)S(1)}, bf16[32,1536]{1,0:T(8,128)(2,1)}, u32[]{:S(2)}) copy-start(bf16[32,1536]{1,0:T(8,128)(2,1)} %param.17) | copy-start | bytes 294916
  7.2 61.0 %collective-permute-start = (bf16[128,576]{0,1:T(8,128)(2,1)}, bf16[128,576]{0,1:T(8,128)(2,1)}, u32[]{:S(2)}, u32[]{:S(2)}) collective-permute-start(bf16[128,576]{0,1:T(8,128)(2,1)} %param.13), channel_id=1, source_target_pairs={{0,64},{8,72},{16,80},{24,88},{32,96},{40,104},{48,112},{56,120},{... | collective-permute-start | bytes 442376 | tf_op jit(solution)/shard_map/ppermute | solution.py:17
  16.9 26.8 %all-to-all-start = ((s32[64,1,2]{2,1,0:T(1,128)}), s32[64,1,2]{2,1,0:T(1,128)}, u32[]{:S(2)}, u32[]{:S(2)}) async-start(s32[64,1,2]{2,1,0:T(1,128)} %stack.2), calls=%async_computation | async-start | bytes 65536 | tf_op jit(solution)/shard_map/all_to_all | solution.py:99
  28.0 185.0 %all-gather.2.cloned.1.call-start = ((), (), s32[]{:S(2)}) async-start(), calls=%async_computation.1 | async-start | bytes 5324800 | tf_op jit(solution)/shard_map/all_gather | solution.py:161
  28.8 796.8 %all-reduce.5.cloned.1.call-start = ((), (), s32[]{:S(2)}) async-start(), calls=%async_computation.2 | async-start | bytes 1703936 | tf_op jit(solution)/shard_map/psum | solution.py:187
  47.5 15.8 %copy-start.67 = (s32[64]{0:T(128)}, s32[64]{0:T(128)S(1)}, u32[]{:S(2)}) copy-start(s32[64]{0:T(128)S(1)} %iota_add_fusion.14) | copy-start | bytes 772
  48.2 15.1 %copy-start.68 = (s32[64]{0:T(128)}, s32[64]{0:T(128)S(1)}, u32[]{:S(2)}) copy-start(s32[64]{0:T(128)S(1)} %iota_add_fusion.15) | copy-start | bytes 772
  73.5 29.5 %copy-start.30 = (bf16[128,32]{0,1:T(8,128)(2,1)}, bf16[128,32]{0,1:T(8,128)(2,1)S(1)}, u32[]{:S(2)}) copy-start(bf16[128,32]{0,1:T(8,128)(2,1)S(1)} %get-tuple-element.30) | copy-start | bytes 24580
  73.5 29.6 %copy-start.32 = (bf16[128,32]{0,1:T(8,128)(2,1)}, bf16[128,32]{0,1:T(8,128)(2,1)S(1)}, u32[]{:S(2)}) copy-start(bf16[128,32]{0,1:T(8,128)(2,1)S(1)} %get-tuple-element.31) | copy-start | bytes 24580
  85.4 17.2 %collective-permute-start.1 = (bf16[128,576]{0,1:T(8,128)(2,1)}, bf16[128,576]{0,1:T(8,128)(2,1)S(1)}, u32[]{:S(2)}, u32[]{:S(2)}) collective-permute-start(bf16[128,576]{0,1:T(8,128)(2,1)} %collective-permute-done), channel_id=1, source_target_pairs={{0,64},{8,72},{16,80},{24,88},{32,96},{40,104},{48,112},{56,120},{... | collective-permute-start | bytes 442376 | tf_op jit(solution)/shard_map/ppermute | solution.py:17
  103.1 17.1 %copy-start.5 = (bf16[128,2048]{1,0:T(8,128)(2,1)}, bf16[128,2048]{1,0:T(8,128)(2,1)S(1)}, u32[]{:S(2)}) copy-start(bf16[128,2048]{1,0:T(8,128)(2,1)S(1)} %convolution_convert_fusion.5) | copy-start | bytes 1572868
  104.3 14.2 %collective-permute-start.2 = (bf16[128,576]{0,1:T(8,128)(2,1)S(1)}, bf16[128,576]{0,1:T(8,128)(2,1)S(1)}, u32[]{:S(2)}, u32[]{:S(2)}) collective-permute-start(bf16[128,576]{0,1:T(8,128)(2,1)S(1)} %collective-permute-done.1), channel_id=1, source_target_pairs={{0,64},{8,72},{16,80},{24,88},{32,96},{40,104},{48,112},{56,120},{... | collective-permute-start | bytes 442376 | tf_op jit(solution)/shard_map/ppermute | solution.py:17
  119.0 16.2 %copy-start.58 = (f32[32]{0:T(128)S(1)}, f32[32]{0:T(128)}, u32[]{:S(2)}) copy-start(f32[32]{0:T(128)} %multiply_power_fusion) | copy-start | bytes 388
  119.0 16.1 %copy-start.63 = (f32[128]{0:T(128)S(1)}, f32[128]{0:T(128)}, u32[]{:S(2)}) copy-start(f32[128]{0:T(128)} %get-tuple-element.79) | copy-start | bytes 1540
  119.0 16.1 %copy-start.64 = (f32[128]{0:T(128)S(1)}, f32[128]{0:T(128)}, u32[]{:S(2)}) copy-start(f32[128]{0:T(128)} %get-tuple-element.80) | copy-start | bytes 1540
  119.0 16.1 %copy-start.74 = (f32[128]{0:T(128)S(1)}, f32[128]{0:T(128)}, u32[]{:S(2)}) copy-start(f32[128]{0:T(128)} %add_convert_fusion.6) | copy-start | bytes 1540
  120.2 12.8 %collective-permute-start.3 = (bf16[128,576]{0,1:T(8,128)(2,1)S(1)}, bf16[128,576]{0,1:T(8,128)(2,1)S(1)}, u32[]{:S(2)}, u32[]{:S(2)}) collective-permute-start(bf16[128,576]{0,1:T(8,128)(2,1)S(1)} %collective-permute-done.2), channel_id=1, source_target_pairs={{0,64},{8,72},{16,80},{24,88},{32,96},{40,104},{48,112},{56,120},{... | collective-permute-start | bytes 442376 | tf_op jit(solution)/shard_map/ppermute | solution.py:17
  136.0 26.1 %copy-start.36 = (bf16[128,32]{0,1:T(8,128)(2,1)}, bf16[128,32]{0,1:T(8,128)(2,1)S(1)}, u32[]{:S(2)}) copy-start(bf16[128,32]{0,1:T(8,128)(2,1)S(1)} %get-tuple-element.24) | copy-start | bytes 24580
  136.0 26.1 %copy-start.38 = (bf16[128,32]{0,1:T(8,128)(2,1)}, bf16[128,32]{0,1:T(8,128)(2,1)S(1)}, u32[]{:S(2)}) copy-start(bf16[128,32]{0,1:T(8,128)(2,1)S(1)} %get-tuple-element.25) | copy-start | bytes 24580
  148.7 12.9 %collective-permute-start.4 = (bf16[128,576]{0,1:T(8,128)(2,1)}, bf16[128,576]{0,1:T(8,128)(2,1)S(1)}, u32[]{:S(2)}, u32[]{:S(2)}) collective-permute-start(bf16[128,576]{0,1:T(8,128)(2,1)} %copy-done.24), channel_id=1, source_target_pairs={{0,64},{8,72},{16,80},{24,88},{32,96},{40,104},{48,112},{56,120},{... | collective-permute-start | bytes 442376 | tf_op jit(solution)/shard_map/ppermute | solution.py:17
  162.1 16.3 %copy-start.4 = (bf16[128,2048]{1,0:T(8,128)(2,1)}, bf16[128,2048]{1,0:T(8,128)(2,1)S(1)}, u32[]{:S(2)}) copy-start(bf16[128,2048]{1,0:T(8,128)(2,1)S(1)} %convolution_convert_fusion.2) | copy-start | bytes 1572868
  162.3 12.5 %collective-permute-start.5 = (bf16[128,576]{0,1:T(8,128)(2,1)S(1)}, bf16[128,576]{0,1:T(8,128)(2,1)S(1)}, u32[]{:S(2)}, u32[]{:S(2)}) collective-permute-start(bf16[128,576]{0,1:T(8,128)(2,1)S(1)} %collective-permute-done.4), channel_id=1, source_target_pairs={{0,64},{8,72},{16,80},{24,88},{32,96},{40,104},{48,112},{56,120},{... | collective-permute-start | bytes 442376 | tf_op jit(solution)/shard_map/ppermute | solution.py:17
  175.2 14.9 %copy-start.59 = (f32[32]{0:T(128)S(1)}, f32[32]{0:T(128)}, u32[]{:S(2)}) copy-start(f32[32]{0:T(128)} %multiply_power_fusion) | copy-start | bytes 388
  175.3 14.9 %copy-start.60 = (f32[128]{0:T(128)S(1)}, f32[128]{0:T(128)}, u32[]{:S(2)}) copy-start(f32[128]{0:T(128)} %get-tuple-element.10) | copy-start | bytes 1540
  175.3 14.9 %copy-start.61 = (f32[128]{0:T(128)S(1)}, f32[128]{0:T(128)}, u32[]{:S(2)}) copy-start(f32[128]{0:T(128)} %get-tuple-element.81) | copy-start | bytes 1540
  175.3 14.9 %copy-start.62 = (f32[128]{0:T(128)S(1)}, f32[128]{0:T(128)}, u32[]{:S(2)}) copy-start(f32[128]{0:T(128)} %get-tuple-element.82) | copy-start | bytes 1540
  175.3 14.9 %copy-start.73 = (f32[128]{0:T(128)S(1)}, f32[128]{0:T(128)}, u32[]{:S(2)}) copy-start(f32[128]{0:T(128)} %add_convert_fusion.9) | copy-start | bytes 1540
  175.4 13.3 %collective-permute-start.6 = (bf16[128,576]{0,1:T(8,128)(2,1)S(1)}, bf16[128,576]{0,1:T(8,128)(2,1)S(1)}, u32[]{:S(2)}, u32[]{:S(2)}) collective-permute-start(bf16[128,576]{0,1:T(8,128)(2,1)S(1)} %collective-permute-done.5), channel_id=1, source_target_pairs={{0,64},{8,72},{16,80},{24,88},{32,96},{40,104},{48,112},{56,120},{... | collective-permute-start | bytes 442376 | tf_op jit(solution)/shard_map/ppermute | solution.py:17
  226.2 56.8 %copy-start.20 = (bf16[128,1536]{1,0:T(8,128)(2,1)S(1)}, bf16[128,1536]{1,0:T(8,128)(2,1)}, u32[]{:S(2)}) copy-start(bf16[128,1536]{1,0:T(8,128)(2,1)} %param.12) | copy-start | bytes 1179652
  226.2 605.6 %copy-start.1 = (bf16[512,2048]{1,0:T(8,128)(2,1)S(1)}, bf16[512,2048]{1,0:T(8,128)(2,1)}, u32[]{:S(2)}) copy-start(bf16[512,2048]{1,0:T(8,128)(2,1)} %param.15) | copy-start | bytes 6291460
  (55 other events, 193.3 us)
Sparse Core Ops, SparseCore 0:
  31.0 127.7 all-gather.1
  285.0 540.5 all-reduce.4
